TPU v7x, 32 devices: a whole 2x2x4 slice. The times are simulated.
32 devices in a mesh: dp: 4 (over z), tm: 2 (over x), head: 4 (over y, core).
Axes of the slice: x: 2, y: 2, z: 4, core: 2. Of those that a mesh axis runs over, the one named last changes fastest.
Arguments:
- frames: bfloat16 [4, 768, 1536], P('dp', 'tm')
- projections: bfloat16 [4, 1536, 1536], P(None, None, 'head')
- kernel: bfloat16 [32, 1536], replicated, may hold values from -1 to 1
- pattern: int32 [4, 12, 12], P('dp', 'tm'), may hold values from -1 to 11, as said below
- cotangent: bfloat16 [4, 768, 1536], P('dp', 'tm'), may hold values from -0.109375 to 0.109375
Outputs:
- encoded: bfloat16 [4, 768, 1536], P('dp', 'tm')
- proj_grad: float32 [4, 1536, 1536], P(None, ('dp', 'tm'), 'head')
- kernel_grad: float32 [32, 1536], P(('dp', 'tm'))
Inputs may be any that keep to these rules, and one draw needn't show every extreme that they name: `pattern`: in each row the strided key blocks come first: phase + j * 1 for j = 0, 1, ..., one phase below 1 for the row, 1 to 12 of them; the remaining entries are -1.
All inputs are finite; a program needn't handle non-finite values.
Results may differ from a plain program's by a relative error of at most 0.04.
Values may be sent and summed in bfloat16 or wider, within the bound.
No kernel may reach another device: no remote copies, remote signals or barrier semaphores. Data moves between devices by JAX's collectives and lax.ppermute only.
A program may use at most 128 MiB of HBM per device.

v0:
```python
import jax
import jax.numpy as jnp
from jax import lax
from jax.sharding import PartitionSpec as P

HD = 96
BLK = 64
KW = 32


def extended_2(array, sides, width):
    for axis, dim in sides:
        peers, length = (lax.axis_size(axis), array.shape[dim])
        up = [(i, (i + 1) % peers) for i in range(peers - 1)]
        down = [(j, i) for i, j in up]
        last = lax.slice_in_dim(array, length - width, length, axis=dim)
        first = lax.slice_in_dim(array, 0, width, axis=dim)
        before = lax.ppermute(last, axis, up)
        after = lax.ppermute(first, axis, down)
        array = jnp.concatenate([before, array, after], axis=dim)
    return array


def key_lists(pattern, first_block, nblocks):
    query_count = pattern.shape[0]
    query_block = first_block + jnp.arange(query_count, dtype=jnp.int32)
    band_blocks = query_block[:, None] + jnp.arange(-1, 2, dtype=jnp.int32)[None, :]
    band_live = (band_blocks >= 0) & (band_blocks < nblocks)
    far_live = (pattern >= 0) & (jnp.abs(pattern - query_block[:, None]) > 1)
    listed = jnp.clip(jnp.concatenate([band_blocks, pattern], axis=1), 0, nblocks - 1)
    live_mask = jnp.concatenate([band_live, far_live], axis=1)
    return (listed, live_mask)


def gather_blocks(source, listed, block_len, head_dim):
    head_count = source.shape[1] // head_dim
    gathered = source.reshape(-1, block_len, head_count, head_dim)[listed]
    return gathered.reshape(listed.shape[0], listed.shape[1] * block_len, head_count, head_dim)


def masked_scores(query_tiles, key_tiles, live_mask, block_len):
    score_scale = query_tiles.shape[-1] ** (-0.5)
    scores = (
        jnp.einsum("qthd,qkhd->qhtk", query_tiles, key_tiles, preferred_element_type=jnp.float32)
        * score_scale
    )
    column_live = jnp.repeat(live_mask, block_len, axis=1)[:, None, None, :]
    return (jnp.where(column_live, scores, -1e30), column_live)


def attend(queries, key_rows, values, listed, live_mask, block_len, head_dim):
    head_count = queries.shape[1] // head_dim
    query_tiles = queries.reshape(listed.shape[0], block_len, head_count, head_dim)
    key_tiles = gather_blocks(key_rows, listed, block_len, head_dim)
    value_tiles = gather_blocks(values, listed, block_len, head_dim)
    scores, column_live = masked_scores(query_tiles, key_tiles, live_mask, block_len)
    highest = jnp.max(scores, axis=-1, keepdims=True)
    logsum = highest + jnp.log(jnp.sum(jnp.exp(scores - highest), axis=-1, keepdims=True))
    weights = jnp.where(column_live, jnp.exp(scores - logsum), 0.0).astype(jnp.bfloat16)
    mixed_rows = jnp.einsum(
        "qhtk,qkhd->qthd", weights, value_tiles, preferred_element_type=jnp.float32
    ).astype(jnp.bfloat16)
    return (mixed_rows.reshape(queries.shape), logsum)


def attend_back(
    queries,
    key_rows,
    values,
    listed,
    live_mask,
    logsum,
    mixed_rows,
    grad_mixed,
    block_len,
    head_dim,
    nblocks,
):
    head_count = queries.shape[1] // head_dim
    shape_tiles = (listed.shape[0], block_len, head_count, head_dim)
    query_tiles = queries.reshape(shape_tiles)
    grad_tiles = grad_mixed.reshape(shape_tiles)
    mixed_tiles = mixed_rows.reshape(shape_tiles)
    key_tiles = gather_blocks(key_rows, listed, block_len, head_dim)
    value_tiles = gather_blocks(values, listed, block_len, head_dim)
    scores, column_live = masked_scores(query_tiles, key_tiles, live_mask, block_len)
    probabilities = jnp.where(column_live, jnp.exp(scores - logsum), 0.0)
    row_delta = jnp.einsum(
        "qthd,qthd->qht", grad_tiles, mixed_tiles, preferred_element_type=jnp.float32
    )
    grad_probs = jnp.einsum(
        "qthd,qkhd->qhtk", grad_tiles, value_tiles, preferred_element_type=jnp.float32
    )
    score_scale = head_dim ** (-0.5)
    grad_scores = (probabilities * (grad_probs - row_delta[..., None]) * score_scale).astype(
        jnp.bfloat16
    )
    grad_queries = jnp.einsum(
        "qhtk,qkhd->qthd", grad_scores, key_tiles, preferred_element_type=jnp.float32
    )
    grad_queries = grad_queries.astype(jnp.bfloat16).reshape(queries.shape)
    weights = probabilities.astype(jnp.bfloat16)
    key_terms = jnp.einsum(
        "qhtk,qthd->qkhd", grad_scores, query_tiles, preferred_element_type=jnp.float32
    )
    value_terms = jnp.einsum(
        "qhtk,qthd->qkhd", weights, grad_tiles, preferred_element_type=jnp.float32
    )
    block_ids = jnp.arange(nblocks, dtype=jnp.int32)
    onehot = (
        (listed.reshape(-1)[:, None] == block_ids[None, :]) & live_mask.reshape(-1)[:, None]
    ).astype(jnp.float32)
    tile_width = block_len * queries.shape[1]
    key_grad = jnp.dot(onehot.T, key_terms.reshape(-1, tile_width), precision=lax.Precision.HIGHEST)
    value_grad = jnp.dot(
        onehot.T, value_terms.reshape(-1, tile_width), precision=lax.Precision.HIGHEST
    )
    key_grad = key_grad.reshape(nblocks * block_len, queries.shape[1])
    value_grad = value_grad.reshape(nblocks * block_len, queries.shape[1])
    return (grad_queries, row_delta, key_grad, value_grad)


def conv_apply(residual, upstream, extended, kernel_cols, frame_count, width, half_width):
    padded = extended[:, :width]
    padded_up = extended[:, width:]
    upstream_wide = upstream.astype(jnp.float32)
    encoded = residual.astype(jnp.float32)
    back_grad = upstream_wide
    taps_grad = []
    for offset in range(2 * half_width):
        weight_row = kernel_cols[offset].astype(jnp.float32)
        shifted = padded[offset : offset + frame_count].astype(jnp.float32)
        encoded = encoded + weight_row * shifted
        back_grad = back_grad + weight_row * padded_up[
            2 * half_width - offset : 2 * half_width - offset + frame_count
        ].astype(jnp.float32)
        taps_grad.append(jnp.sum(upstream_wide * shifted, axis=0))
    return (encoded.astype(jnp.bfloat16), back_grad.astype(jnp.bfloat16), jnp.stack(taps_grad))


def shards(frames, projections, kernel, pattern, cotangent):
    source = frames[0]
    upstream = cotangent[0]
    rows_pattern = pattern[0]
    frame_count = source.shape[0]
    model_width = source.shape[1]
    head_width = projections.shape[2]
    local_blocks = frame_count // BLK
    cycle_size = lax.axis_size("tm")
    nblocks = local_blocks * cycle_size
    first_block = lax.axis_index("tm") * local_blocks
    half_width = KW // 2
    contract = (((0,), (0,)), ((), ()))
    listed, live_mask = key_lists(rows_pattern, first_block, nblocks)
    queries = jnp.dot(source, projections[0], preferred_element_type=jnp.float32).astype(
        jnp.bfloat16
    )
    key_rows = jnp.dot(source, projections[1], preferred_element_type=jnp.float32).astype(
        jnp.bfloat16
    )
    values = jnp.dot(source, projections[2], preferred_element_type=jnp.float32).astype(
        jnp.bfloat16
    )
    key_all, value_all = (
        lax.all_gather(key_rows, "tm", axis=0, tiled=True),
        lax.all_gather(values, "tm", axis=0, tiled=True),
    )
    mixed_rows, logsum = attend(queries, key_all, value_all, listed, live_mask, BLK, HD)
    output_part = lax.dot_general(
        mixed_rows, projections[3], (((1,), (1,)), ((), ())), preferred_element_type=jnp.float32
    )
    summed = lax.psum(output_part.astype(jnp.bfloat16), "head").astype(jnp.float32)
    residual = (source.astype(jnp.float32) + summed).astype(jnp.bfloat16)
    extended = extended_2(jnp.concatenate([residual, upstream], axis=1), (("tm", 0),), half_width)
    encoded, back_grad, kernel_grad = conv_apply(
        residual, upstream, extended, kernel, frame_count, model_width, half_width
    )
    grad_mixed = jnp.dot(back_grad, projections[3], preferred_element_type=jnp.float32).astype(
        jnp.bfloat16
    )
    grad_queries, row_delta, key_grad, value_grad = attend_back(
        queries,
        key_all,
        value_all,
        listed,
        live_mask,
        logsum,
        mixed_rows,
        grad_mixed,
        BLK,
        HD,
        nblocks,
    )
    key_value_terms = jnp.concatenate([key_grad, value_grad], axis=1)
    owned = lax.psum_scatter(
        key_value_terms.astype(jnp.bfloat16), "tm", scatter_dimension=0, tiled=True
    ).astype(jnp.float32)
    key_own = owned[:, :head_width].astype(jnp.bfloat16)
    value_own = owned[:, head_width:].astype(jnp.bfloat16)
    proj_grad = jnp.stack(
        [
            lax.dot_general(source, grad_queries, contract, preferred_element_type=jnp.float32),
            lax.dot_general(source, key_own, contract, preferred_element_type=jnp.float32),
            lax.dot_general(source, value_own, contract, preferred_element_type=jnp.float32),
            lax.dot_general(back_grad, mixed_rows, contract, preferred_element_type=jnp.float32),
        ]
    )
    proj_result, kernel_result = (
        lax.psum_scatter(
            proj_grad.astype(jnp.bfloat16), ("dp", "tm"), scatter_dimension=1, tiled=True
        ).astype(jnp.float32),
        lax.psum_scatter(
            kernel_grad.astype(jnp.bfloat16), ("dp", "tm"), scatter_dimension=0, tiled=True
        ).astype(jnp.float32),
    )
    return (encoded[None], proj_result, kernel_result)


def solution(mesh):
    placed = (
        P("dp", "tm", None),
        P(None, None, "head"),
        P(),
        P("dp", "tm", None),
        P("dp", "tm", None),
    )
    return jax.shard_map(
        shards,
        mesh=mesh,
        in_specs=placed,
        out_specs=(P("dp", "tm", None), P(None, ("dp", "tm"), "head"), P(("dp", "tm"), None)),
        check_vma=False,
    )
```

profile of v0, /device:TPU:0, one launch (start us, length us, event | category | flops | bytes accessed | tf_op | source)
XLA Modules:
  0.0 487.5 jit_solution(7557210510421233917)
XLA Ops:
  14.8 10.6 %all_gather.6 = bf16[768,384]{1,0:T(8,128)(2,1)S(1)} all-gather(bf16[384,384]{1,0:T(8,128)(2,1)S(1)} %convolution_convert_fusion.10), channel_id=1, replica_groups=mesh['dp'=4,'tm'=2,'head'=4] {'tm'}, dimensions={0}, use_global_device_ids=true | all-gather | bytes 884736 | tf_op jit(solution)/shard_map/all_gather | solution.py:166
  26.3 9.3 %all_gather.7 = bf16[768,384]{1,0:T(8,128)(2,1)S(1)} all-gather(bf16[384,384]{1,0:T(8,128)(2,1)S(1)} %convolution_convert_fusion.8), channel_id=1, replica_groups=mesh['dp'=4,'tm'=2,'head'=4] {'tm'}, dimensions={0}, use_global_device_ids=true | all-gather | bytes 884736 | tf_op jit(solution)/shard_map/all_gather | solution.py:165
  36.4 5.8 %gather_fusion.1 = bf16[90,64,4,96]{3,1,2,0:T(8,128)(2,1)} fusion(bf16[12,64,4,96]{3,1,2,0:T(8,128)(2,1)S(1)} %copy.56, s32[1024]{0:T(1024)S(1)} %pad_clamp_fusion), kind=kCustom, calls=%fused_computation.1 | custom fusion | bytes 8847720 | tf_op jit(solution)/shard_map/gather | solution.py:37
  42.2 7.1 %copy.57 = bf16[90,64,4,96]{3,1,0,2:T(8,128)(2,1)} copy(bf16[90,64,4,96]{3,1,2,0:T(8,128)(2,1)} %gather_fusion.1) | data formatting | bytes 8847360 | tf_op jit(solution)/shard_map/gather | solution.py:37
  49.3 5.8 %gather_fusion = bf16[90,64,4,96]{3,1,2,0:T(8,128)(2,1)} fusion(bf16[12,64,4,96]{3,1,2,0:T(8,128)(2,1)S(1)} %copy.54, s32[1024]{0:T(1024)S(1)} %pad_clamp_fusion), kind=kCustom, calls=%fused_computation | custom fusion | bytes 8847720 | tf_op jit(solution)/shard_map/gather | solution.py:37
  55.1 4.3 copy.55
  72.8 36.6 %all-reduce.6.cloned.1.call-done = bf16[384,1536]{1,0:T(8,128)(2,1)} async-done(((bf16[384,1536]{1,0:T(8,128)(2,1)}), bf16[384,1536]{1,0:T(8,128)(2,1)}) %all-reduce.6.cloned.1.call-update) | async-done | bytes 1179664 | tf_op jit(solution)/shard_map/psum | solution.py:172
  116.7 4.3 collective-permute-done.1
  122.9 5.7 %fusion.86 = (bf16[1536]{0:T(1024)(128)(2,1)}, bf16[1536]{0:T(1024)(128)(2,1)}, bf16[1536]{0:T(1024)(128)(2,1)}, bf16[1536]{0:T(1024)(128)(2,1)}, bf16[1536]{0:T...) fusion(bf16[400,3072]{1,0:T(8,128)(2,1)S(1)} %get-tuple-element, ...), kind=kLoop, calls=%fused_computation.171 | loop fusion | flops 28876800 | bytes 20103168 | tf_op jit(solution)/shard_map/reduce_sum | solution.py:137
  128.9 10.0 %add_convert_fusion = bf16[384,1536]{1,0:T(8,128)(2,1)S(1)} fusion(bf16[400,3072]{1,0:T(8,128)(2,1)S(1)} %get-tuple-element.81, bf16[400,3072]{1,0:T(8,128)(2,1)S(1)} %get-tuple-element.82, f32[1536]{0:T(1024)S(1)} %get-tuple-element.77, f32[1536]{0:T(1024)S(1)} %get-tuple-element.78, f32[1536]{0:T(1024)S(1)} %copy-done.18, f32[1536]{0:T(1024)S(1)} %copy-done.20, ...), kind=kLoop, calls=%fused_computation.188 | loop fusion | flops 57212928 | bytes 39124992 | tf_op jit(solution)/shard_map/convert_element_type | solution.py:138
  144.1 8.5 %convolution_bitcast_fusion = f32[6,960,4,96]{1,3,2,0:T(8,128)} fusion(bf16[6,64,4,96]{3,2,1,0:T(4,128)(2,1)S(1)} %reshape.155, f32[6,4,64,960]{3,2,1,0:T(8,128)} %copy-done.1, f32[6,4,64]{2,1,0:T(4,128)} %bitcast.127, pred[6,960]{1,0:T(8,128)(4,1)S(1)} %broadcast_in_dim.33), kind=kOutput, calls=%fused_computation.55 | convolution fusion | flops 290488320 | bytes 15052416 | tf_op jit(solution)/shard_map/qhtk,qthd->qkhd/dot_general | solution.py:106
  166.5 13.3 %copy.69 = f32[6,960,4,96]{3,2,1,0:T(4,128)} copy(f32[6,960,4,96]{1,3,2,0:T(8,128)} %convolution_bitcast_fusion) | data formatting | bytes 17694720 | tf_op jit(solution)/shard_map/qhtk,qthd->qkhd/transpose | solution.py:106
  179.8 15.5 %reshape.159 = f32[90,24576]{1,0:T(8,128)} reshape(f32[6,960,4,96]{3,2,1,0:T(4,128)} %copy.69) | data formatting | bytes 17694720 | tf_op jit(solution)/shard_map/reshape | solution.py:116
  195.3 7.7 %convolution_convert_fusion = bf16[12,24576]{1,0:T(8,128)(2,1)} fusion(f32[90,24576]{1,0:T(8,128)} %reshape.159, s32[90]{0:T(128)S(1)} %copy-done.100, pred[90]{0:T(512)(128)(4,1)S(1)} %copy-done.101), kind=kOutput, calls=%fused_computation.2 | convolution fusion | flops 318802048 | bytes 9437634 | tf_op jit(solution)/shard_map/dot_general | solution.py:115
  205.5 6.8 %convolution_bitcast_fusion.1 = f32[6,960,4,96]{1,3,2,0:T(8,128)} fusion(bf16[6,4,64,960]{3,2,1,0:T(8,128)(2,1)} %multiply_convert_fusion, bf16[6,64,4,96]{3,2,1,0:T(4,128)(2,1)S(1)} %reshape.151), kind=kOutput, calls=%fused_computation.56 | convolution fusion | flops 283115520 | bytes 12091392 | tf_op jit(solution)/shard_map/qhtk,qthd->qkhd/dot_general | solution.py:103
  212.3 13.3 %copy.67 = f32[6,960,4,96]{3,2,1,0:T(4,128)} copy(f32[6,960,4,96]{1,3,2,0:T(8,128)} %convolution_bitcast_fusion.1) | data formatting | bytes 17694720 | tf_op jit(solution)/shard_map/qhtk,qthd->qkhd/transpose | solution.py:103
  225.6 15.3 %reshape.157 = f32[90,24576]{1,0:T(8,128)} reshape(f32[6,960,4,96]{3,2,1,0:T(4,128)} %copy.67) | data formatting | bytes 17694720 | tf_op jit(solution)/shard_map/reshape | solution.py:114
  240.9 6.8 %convolution_convert_fusion.1 = bf16[12,24576]{1,0:T(8,128)(2,1)S(1)} fusion(f32[90,24576]{1,0:T(8,128)} %reshape.157, s32[90]{0:T(128)S(1)} %copy-done.100, pred[90]{0:T(512)(128)(4,1)S(1)} %copy-done.101), kind=kOutput, calls=%fused_computation.3 | convolution fusion | flops 318802048 | bytes 9437634 | tf_op jit(solution)/shard_map/dot_general | solution.py:114
  251.5 13.3 %fusion.102 = (bf16[1536]{0:T(1024)(128)(2,1)S(1)}, bf16[1536]{0:T(1024)(128)(2,1)S(1)}, bf16[1536]{0:T(1024)(128)(2,1)S(1)}, bf16[1536]{0:T(1024)(128)(2,1)S(1)...) fusion(bf16[400,3072]{1,0:T(8,128)(2,1)} %copy-done, ...), kind=kLoop, calls=%fused_computation.187 | loop fusion | flops 28876800 | bytes 20103168 | tf_op jit(solution)/shard_map/reduce_sum | solution.py:137
  274.3 4.0 fusion.111
  278.9 5.9 %stack.189 = bf16[32,1536]{1,0:T(8,128)(2,1)} concatenate(bf16[1,1536]{1,0:T(2,128)(2,1)} %stack.157, bf16[1,1536]{1,0:T(2,128)(2,1)} %stack.158, bf16[1,1536]{1,0:T(2,128)(2,1)} %stack.159, bf16[1,1536]{1,0:T(2,128)(2,1)} %stack.160, bf16[1,1536]{1,0:T(2,128)(2,1)} %stack.161, bf16[1,1536]{1,0:T(2,128)(2,1)} %stack.162, bf16[1,1536]{1,0:T(2,128)(2,1)} %stack.163, ...), dimensions={0} | concatenate | bytes 196608 | tf_op jit(solution)/shard_map/stack | solution.py:138
  296.4 8.5 %copy.71 = bf16[4,1536,384]{2,0,1:T(4,128)(2,1)} copy(bf16[4,1536,384]{1,2,0:T(8,128)(2,1)} %pad_maximum_fusion) | data formatting | bytes 9437184 | tf_op jit(solution)/shard_map/stack | solution.py:200
  307.8 20.4 %fusion.128 = bf16[1,384,1536]{2,1,0:T(8,128)(2,1)} fusion(f32[1536]{0:T(1024)S(1)} %copy-done.77, f32[1536]{0:T(1024)S(1)} %copy-done.79, f32[1536]{0:T(1024)S(1)} %copy-done.19, f32[1536]{0:T(1024)S(1)} %copy-done.21, f32[1536]{0:T(1024)S(1)} %copy-done.23, f32[1536]{0:T(1024)S(1)} %copy-done.25, f32[1536]{0:T(1024)S(1)} %copy-done.27, ...), kind=kLoop, calls=%fused_computation.212 | loop fusion | flops 57212928 | bytes 39124992 | tf_op jit(solution)/shard_map/broadcast_in_dim | solution.py:216
  328.2 148.7 %all-reduce.8.cloned.1.call-done = (bf16[4,1536,384]{2,0,1:T(4,128)(2,1)}, bf16[32,1536]{1,0:T(8,128)(2,1)}) async-done(((bf16[4,1536,384]{2,0,1:T(4,128)(2,1)}, bf16[32,1536]{1,0:T(8,128)(2,1)}), (bf16[4,1536,384]{2,0,1:T(4,128)(2,1)}, bf16[32,1536]{1,0:T(8,128)(2,1)})) %all-reduce.8.cloned.1.call-update) | async-done | bytes 4816912
  (313 shorter events, 82.8 us)
Async XLA Ops:
  7.2 102.3 %all-reduce.6.cloned.1.call-start = ((), (), s32[]{:S(2)}) async-start(), calls=%async_computation.1 | async-start | bytes 2359296 | tf_op jit(solution)/shard_map/psum | solution.py:172
  66.9 42.6 %copy-start.7 = (bf16[1,384,1536]{2,1,0:T(8,128)(2,1)S(1)}, bf16[1,384,1536]{2,1,0:T(8,128)(2,1)}, u32[]{:S(2)}) copy-start(bf16[1,384,1536]{2,1,0:T(8,128)(2,1)} %param.5) | copy-start | bytes 3538948
  70.4 40.8 %copy-start.2 = (bf16[1,384,1536]{2,1,0:T(8,128)(2,1)S(1)}, bf16[1,384,1536]{2,1,0:T(8,128)(2,1)}, u32[]{:S(2)}) copy-start(bf16[1,384,1536]{2,1,0:T(8,128)(2,1)} %param.9) | copy-start | bytes 3538948
  70.4 219.4 %reduce-scatter.2.cloned.1.call-start = ((), (), s32[]{:S(2)}) async-start(), calls=%async_computation.2 | async-start | bytes 1769472 | tf_op jit(solution)/shard_map/reduce_scatter | solution.py:195
  111.2 5.6 %collective-permute-start = (bf16[16,3072]{1,0:T(8,128)(2,1)S(1)}, bf16[16,3072]{1,0:T(8,128)(2,1)S(1)}, u32[]{:S(2)}, u32[]{:S(2)}) collective-permute-start(bf16[16,3072]{1,0:T(8,128)(2,1)S(1)} %get-tuple-element.83), channel_id=1, source_target_pairs={{0,4},{1,5},{2,6},{3,7},{8,12},{9,13},{10,14},{11,15},{16,20},{17,... | collective-permute-start | bytes 294920 | tf_op jit(solution)/shard_map/ppermute | solution.py:18
  114.5 6.5 %collective-permute-start.1 = (bf16[16,3072]{1,0:T(8,128)(2,1)S(1)}, bf16[16,3072]{1,0:T(8,128)(2,1)S(1)}, u32[]{:S(2)}, u32[]{:S(2)}) collective-permute-start(bf16[16,3072]{1,0:T(8,128)(2,1)S(1)} %get-tuple-element.84), channel_id=1, source_target_pairs={{4,0},{5,1},{6,2},{7,3},{12,8},{13,9},{14,10},{15,11},{20,16},{21,... | collective-permute-start | bytes 294920 | tf_op jit(solution)/shard_map/ppermute | solution.py:19
  143.8 18.7 %slice-start = ((s8[6291456]{0:T(1024)(128)(4,1)}), s8[4194304]{0:T(1024)(128)(4,1)S(1)}, s32[]{:S(2)}) async-start(s8[6291456]{0:T(1024)(128)(4,1)} %bitcast.113), calls=%async_computation.4 | async-start | bytes 8388608
  143.8 18.7 %slice-start.2 = ((s8[5898240]{0:T(1024)(128)(4,1)}), s8[4194304]{0:T(1024)(128)(4,1)S(1)}, s32[]{:S(2)}) async-start(s8[5898240]{0:T(1024)(128)(4,1)} %bitcast.120), calls=%async_computation.6 | async-start | bytes 8388608
  144.0 13.4 %copy-start.91 = (bf16[1536]{0:T(1024)(128)(2,1)S(1)}, bf16[1536]{0:T(1024)(128)(2,1)}, u32[]{:S(2)}) copy-start(bf16[1536]{0:T(1024)(128)(2,1)} %get-tuple-element.38) | copy-start | bytes 9220
  144.0 14.0 %copy-start.90 = (bf16[1536]{0:T(1024)(128)(2,1)S(1)}, bf16[1536]{0:T(1024)(128)(2,1)}, u32[]{:S(2)}) copy-start(bf16[1536]{0:T(1024)(128)(2,1)} %get-tuple-element.39) | copy-start | bytes 9220
  144.0 14.6 %copy-start.89 = (bf16[1536]{0:T(1024)(128)(2,1)S(1)}, bf16[1536]{0:T(1024)(128)(2,1)}, u32[]{:S(2)}) copy-start(bf16[1536]{0:T(1024)(128)(2,1)} %get-tuple-element.40) | copy-start | bytes 9220
  144.0 15.2 %copy-start.88 = (bf16[1536]{0:T(1024)(128)(2,1)S(1)}, bf16[1536]{0:T(1024)(128)(2,1)}, u32[]{:S(2)}) copy-start(bf16[1536]{0:T(1024)(128)(2,1)} %get-tuple-element.41) | copy-start | bytes 9220
  144.0 15.8 %copy-start.87 = (bf16[1536]{0:T(1024)(128)(2,1)S(1)}, bf16[1536]{0:T(1024)(128)(2,1)}, u32[]{:S(2)}) copy-start(bf16[1536]{0:T(1024)(128)(2,1)} %get-tuple-element.42) | copy-start | bytes 9220
  144.0 16.4 %copy-start.86 = (bf16[1536]{0:T(1024)(128)(2,1)S(1)}, bf16[1536]{0:T(1024)(128)(2,1)}, u32[]{:S(2)}) copy-start(bf16[1536]{0:T(1024)(128)(2,1)} %get-tuple-element.43) | copy-start | bytes 9220
  144.1 17.0 %copy-start.85 = (bf16[1536]{0:T(1024)(128)(2,1)S(1)}, bf16[1536]{0:T(1024)(128)(2,1)}, u32[]{:S(2)}) copy-start(bf16[1536]{0:T(1024)(128)(2,1)} %get-tuple-element.44) | copy-start | bytes 9220
  144.1 17.5 %copy-start.84 = (bf16[1536]{0:T(1024)(128)(2,1)S(1)}, bf16[1536]{0:T(1024)(128)(2,1)}, u32[]{:S(2)}) copy-start(bf16[1536]{0:T(1024)(128)(2,1)} %get-tuple-element.45) | copy-start | bytes 9220
  144.1 18.1 %copy-start.16 = (bf16[6,4,96,64]{2,3,1,0:T(8,128)(2,1)S(1)}, bf16[6,4,96,64]{2,3,1,0:T(8,128)(2,1)}, u32[]{:S(2)}) copy-start(bf16[6,4,96,64]{2,3,1,0:T(8,128)(2,1)} %copy-done.15) | copy-start | bytes 884740
  144.1 18.4 %slice-start.1 = ((s8[6291456]{0:T(1024)(128)(4,1)}), s8[2097152]{0:T(1024)(128)(4,1)S(1)}, s32[]{:S(2)}) async-start(s8[6291456]{0:T(1024)(128)(4,1)} %bitcast.113), calls=%async_computation.5 | async-start | bytes 4194304
  144.1 18.4 %slice-start.3 = ((s8[5898240]{0:T(1024)(128)(4,1)}), s8[1703936]{0:T(1024)(128)(4,1)S(1)}, s32[]{:S(2)}) async-start(s8[5898240]{0:T(1024)(128)(4,1)} %bitcast.120), calls=%async_computation.7 | async-start | bytes 3407872
  144.1 18.4 %copy-start.81 = (f32[3,8,64]{2,1,0:T(8,128)S(1)}, f32[3,8,64]{2,1,0:T(8,128)}, u32[]{:S(2)}) copy-start(f32[3,8,64]{2,1,0:T(8,128)} %copy-done.80) | copy-start | bytes 18436
  179.8 15.5 %copy-start.100 = (s32[90]{0:T(128)S(1)}, s32[90]{0:T(128)}, u32[]{:S(2)}) copy-start(s32[90]{0:T(128)} %min.18) | copy-start | bytes 1084
  179.8 15.5 %copy-start.101 = (pred[90]{0:T(512)(128)(4,1)S(1)}, pred[90]{0:T(512)(128)(4,1)}, u32[]{:S(2)}) copy-start(pred[90]{0:T(512)(128)(4,1)} %and.19) | copy-start | bytes 274
  251.4 225.4 %all-reduce.8.cloned.1.call-start = ((), (), s32[]{:S(2)}) async-start(), calls=%async_computation.3 | async-start | bytes 9633792
  251.5 22.8 %copy-start.11 = (bf16[6,4,64,960]{3,2,1,0:T(8,128)(2,1)S(1)}, bf16[6,4,64,960]{3,2,1,0:T(8,128)(2,1)}, u32[]{:S(2)}) copy-start(bf16[6,4,64,960]{3,2,1,0:T(8,128)(2,1)} %multiply_convert_fusion) | copy-start | bytes 8847364
  (88 other events, 512.3 us)
Sparse Core Ops, SparseCore 0:
  70.5 38.8 all-reduce.5
  251.5 21.0 reduce-scatter.1
  305.3 171.4 all-reduce.7
where the time goes:
time: 492 us; the launch traced here: 488 us
  waiting for transfers between devices  190 us (39%)
  local copies, waits for them, and re-layouts  128 us (26%)
  matrix products  63.8 us (13%)
  other arithmetic  63.5 us (13%)
  blocking collectives  19.9 us (4%)
  between operations  17.2 us (3%)
  starting transfers between devices  4.96 us (1%)
    unnamed x4, waiting for transfers between devices  149 us
    psum x1, waiting for transfers between devices, shards(): lax.psum(output_part.astype(jnp.bfloat16), 'head').astype(jnp.float32)  36.6 us
    another operation x33, local copies, waits for them, and re-layouts, conv_apply(): jnp.stack(taps_grad)  25 us
    gather x4, local copies, waits for them, and re-layouts, gather_blocks(): gathered = source.reshape(-1, block_len, head_count, head_dim)[listed]  23 us
    broadcast_in_dim x1, other arithmetic, shards(): return (encoded[None], proj_result, kernel_result)  20.4 us
    reduce_sum x2, other arithmetic, conv_apply(): taps_grad.append(jnp.sum(upstream_wide * shifted, axis=0))  18.9 us
    reshape x1, local copies, waits for them, and re-layouts, attend_back(): value_terms.reshape(-1, tile_width)  15.5 us
    reshape x1, local copies, waits for them, and re-layouts, attend_back(): key_terms.reshape(-1, tile_width)  15.3 us
  transfers between devices with their start and end apart: 5, of which 4 were waited for; matrix products, arithmetic and copies ran while one was open for 13% of the time, Pallas kernels for 0%

commit v1 on v0

--- a/solution.py
+++ b/solution.py
@@ -1,7 +1,12 @@
+import functools
+
 import jax
 import jax.numpy as jnp
 from jax import lax
+from jax.experimental import pallas as pl
+from jax.experimental.pallas import tpu as pltpu
 from jax.sharding import PartitionSpec as P
+
 
 HD = 96
 BLK = 64
@@ -178,7 +183,7 @@
     grad_mixed = jnp.dot(back_grad, projections[3], preferred_element_type=jnp.float32).astype(
         jnp.bfloat16
     )
-    grad_queries, row_delta, key_grad, value_grad = attend_back(
+    grad_queries, _, key_grad, value_grad = attend_back(
         queries,
         key_all,
         value_all,
@@ -216,6 +221,563 @@
     return (encoded[None], proj_result, kernel_result)
 
 
+NN = (((1,), (0,)), ((), ()))
+NT = (((1,), (1,)), ((), ()))
+TN = (((0,), (0,)), ((), ()))
+LANES = 128
+EDGE = KW // 2
+BF16 = jnp.bfloat16
+F32 = jnp.float32
+
+
+def dot32(left, right, dims):
+    return lax.dot_general(left, right, dims, preferred_element_type=F32)
+
+
+def shape(*dims, dtype=BF16):
+    return jax.ShapeDtypeStruct(dims, dtype)
+
+
+def run(body, outs, flops, *args, **options):
+    scalar = pl.BlockSpec(memory_space=pltpu.SMEM)
+    whole = pl.BlockSpec(memory_space=pltpu.VMEM)
+    options.setdefault("in_specs", [scalar] + [whole] * (len(args) - 1))
+    moved = sum(int(x.size) * x.dtype.itemsize for x in args)
+    return pl.pallas_call(
+        body,
+        out_shape=outs,
+        compiler_params=pltpu.CompilerParams(vmem_limit_bytes=40 << 20),
+        cost_estimate=pl.CostEstimate(flops=flops, bytes_accessed=moved, transcendentals=0),
+        **options,
+    )(*args)
+
+
+def pack(array):
+    rows = array.shape[0] // 2
+    return jnp.concatenate([array[:rows], array[rows:]], axis=1)
+
+
+def unpack(array):
+    width = array.shape[1] // 2
+    return jnp.concatenate([array[:, :width], array[:, width:]], axis=0)
+
+
+def project_kernel(meta, source, weights, own_ref, send_ref):
+    whole = dot32(source[...], weights[0], NN).astype(BF16)
+    width = whole.shape[1] // 2
+    low, high = (whole[:, :width], whole[:, width:])
+    first = meta[0] == 0
+    own_ref[0] = jnp.where(first, low, high)
+    send_ref[0] = pack(jnp.where(first, high, low))
+
+
+def project(meta, source, projections):
+    count, width = source.shape
+    cols = projections.shape[2]
+    return run(
+        project_kernel,
+        (shape(3, count, cols // 2), shape(3, count // 2, cols)),
+        6 * count * width * cols,
+        meta,
+        source,
+        projections,
+        grid=(3,),
+        in_specs=[
+            pl.BlockSpec(memory_space=pltpu.SMEM),
+            pl.BlockSpec((count, width), lambda i: (0, 0)),
+            pl.BlockSpec((1, width, cols), lambda i: (i, 0, 0)),
+        ],
+        out_specs=(
+            pl.BlockSpec((1, count, cols // 2), lambda i: (i, 0, 0)),
+            pl.BlockSpec((1, count // 2, cols), lambda i: (i, 0, 0)),
+        ),
+    )
+
+
+def conv_rows(rows):
+    return next(size for size in (64, 48, 32, 16) if rows % size == 0)
+
+
+def fill_padded(padded, rows, halo, upper):
+    count = rows.shape[0]
+    padded[0:EDGE] = jnp.where(upper, halo, 0.0)
+    padded[EDGE : EDGE + count] = rows
+    padded[EDGE + count : 2 * EDGE + count] = jnp.where(upper, 0.0, halo)
+
+
+def fill_taps(wide, taps):
+    for offset in range(KW):
+        wide[offset] = jnp.broadcast_to(taps[offset : offset + 1], (8, LANES))
+
+
+def tapped(total, wide, offset, shifted):
+    parts = (shifted.shape[0] // 8, 8, LANES)
+    return total + (wide[offset][None] * shifted.reshape(parts)).reshape(shifted.shape)
+
+
+def back_kernel(meta, up_ref, arrived, taps_ref, weights, back_ref, own_ref, send_ref, padded, wide, sums):
+    count, width = up_ref.shape
+    step = conv_rows(count)
+    upper = meta[0] == 1
+    for chunk in range(width // LANES):
+        cols = slice(chunk * LANES, (chunk + 1) * LANES)
+        rows = up_ref[:, cols].astype(F32)
+        fill_padded(padded, rows, arrived[:, cols].astype(F32), upper)
+        fill_taps(wide, taps_ref[:, cols].astype(F32))
+
+        def body(tile, carry, cols=cols):
+            start = pl.multiple_of(tile * step, step)
+            total = padded[pl.ds(start + EDGE, step)]
+            for phase in range(8):
+                loaded = padded[pl.ds(start + phase + 1, step + KW - 8)]
+                for block in range(KW // 8):
+                    shifted = loaded[8 * block : 8 * block + step]
+                    total = tapped(total, wide, KW - 1 - phase - 8 * block, shifted)
+            back_ref[pl.ds(start, step), cols] = total.astype(BF16)
+            return carry
+
+        lax.fori_loop(0, count // step, body, 0)
+        part = dot32(back_ref[:, cols], weights[0, cols, :], NN)
+        sums[...] = part if chunk == 0 else sums[...] + part
+    grad = sums[...].astype(BF16)
+    half = grad.shape[1] // 2
+    low, high = (grad[:, :half], grad[:, half:])
+    own_ref[...] = jnp.where(upper, high, low)
+    send_ref[...] = pack(jnp.where(upper, low, high))
+
+
+def back_conv(meta, upstream, arrived, taps, projections):
+    count, width = upstream.shape
+    cols = projections.shape[2]
+    whole = pl.BlockSpec(memory_space=pltpu.VMEM)
+    return run(
+        back_kernel,
+        (shape(count, width), shape(count, cols // 2), shape(count // 2, cols)),
+        2 * count * width * cols + 80 * KW * count * width,
+        meta,
+        upstream,
+        arrived,
+        taps,
+        projections,
+        grid=(1,),
+        in_specs=[pl.BlockSpec(memory_space=pltpu.SMEM)]
+        + [whole] * 3
+        + [pl.BlockSpec((1, width, cols), lambda i: (3, 0, 0))],
+        out_specs=(whole, whole, whole),
+        scratch_shapes=[
+            pltpu.VMEM((count + KW + 8, LANES), F32),
+            pltpu.VMEM((KW, 8, LANES), F32),
+            pltpu.VMEM((count, cols), F32),
+        ],
+    )
+
+
+def head_parts(own, far, head):
+    width = own.shape[2]
+    cols = slice(head * HD, (head + 1) * HD)
+    late = slice(width + head * HD, width + (head + 1) * HD)
+    return [
+        (own[i, :, cols], jnp.concatenate([far[i, :, cols], far[i, :, late]], axis=0))
+        for i in range(own.shape[0])
+    ]
+
+
+def biased_scores(keys, query, bias):
+    blocks, count = bias.shape
+    wide = jnp.broadcast_to(bias[:, None, :], (blocks, BLK, count)).reshape(blocks * BLK, count)
+    return dot32(keys, query, NT) * HD ** (-0.5) + wide
+
+
+def forward_kernel(meta, bias_ref, own, far, mixed_own, mixed_far, send_ref, logsum_ref):
+    half, width = mixed_own.shape
+    first = meta[0] == 0
+    for head in range(width // HD):
+        cols = slice(head * HD, (head + 1) * HD)
+        queries, keys, vals = head_parts(own, far, head)
+        keys = jnp.concatenate(keys, axis=0)
+        vals = jnp.concatenate(vals, axis=0)
+        for part, mixed_out in enumerate((mixed_own, mixed_far)):
+            span = slice(part * half, (part + 1) * half)
+            scores = biased_scores(keys, queries[part], bias_ref[:, span])
+            highest = jnp.max(scores, axis=0, keepdims=True)
+            powers = jnp.exp(scores - highest)
+            total = jnp.sum(powers, axis=0, keepdims=True)
+            weights = (powers * (1.0 / total)).astype(BF16)
+            mixed_out[:, cols] = dot32(vals, weights, TN).T.astype(BF16)
+            logsum_ref[head : head + 1, span] = highest + jnp.log(total)
+    send_ref[: half // 2] = pack(mixed_far[...])
+    edge = jnp.where(first, mixed_own[half - EDGE :], mixed_own[:EDGE])
+    send_ref[half // 2 :] = jnp.concatenate([edge, edge], axis=1)
+
+
+def backward_kernel(
+    meta, bias_ref, logsum_ref, own, far, grad_own, grad_far, mixed_own, mixed_far, terms_own, terms_far
+):
+    half, width = mixed_own.shape
+    for head in range(width // HD):
+        cols = slice(head * HD, (head + 1) * HD)
+        queries, keys, vals = head_parts(own, far, head)
+        keys = jnp.concatenate(keys, axis=0)
+        vals = jnp.concatenate(vals, axis=0)
+        late = slice(width + head * HD, width + (head + 1) * HD)
+        grads = (grad_own[:, cols], jnp.concatenate([grad_far[:, cols], grad_far[:, late]], axis=0))
+        key_grad = jnp.zeros((2 * half, HD), F32)
+        value_grad = jnp.zeros((2 * half, HD), F32)
+        for part, (mixed, terms) in enumerate(((mixed_own, terms_own), (mixed_far, terms_far))):
+            span = slice(part * half, (part + 1) * half)
+            query, grad = (queries[part], grads[part])
+            scores = biased_scores(keys, query, bias_ref[:, span])
+            prob = jnp.exp(scores - logsum_ref[head : head + 1, span])
+            weights = prob.astype(BF16)
+            product = grad.astype(F32) * mixed[:, cols].astype(F32)
+            delta = jnp.sum(product.T, axis=0, keepdims=True)
+            grad_prob = dot32(vals, grad, NT)
+            grad_scores = (prob * (grad_prob - delta) * HD ** (-0.5)).astype(BF16)
+            terms[:, cols] = dot32(keys, grad_scores, TN).T.astype(BF16)
+            key_grad = key_grad + dot32(grad_scores, query, NN)
+            value_grad = value_grad + dot32(weights, grad, NN)
+        for part, terms in enumerate((terms_own, terms_far)):
+            rows = slice(part * half, (part + 1) * half)
+            terms[:, width + head * HD : width + (head + 1) * HD] = key_grad[rows].astype(BF16)
+            terms[:, 2 * width + head * HD : 2 * width + (head + 1) * HD] = value_grad[rows].astype(BF16)
+
+
+def output_kernel(meta, mixed_own, mixed_far, got, weights, rows_ref, keep_ref, send_ref):
+    half, width = mixed_own.shape
+    first, low_core = (meta[0] == 0, meta[1] % 2 == 0)
+    far = mixed_far[...]
+    mine = jnp.concatenate(
+        [mixed_own[...], jnp.where(first, far[:EDGE], far[half - EDGE :])], axis=0
+    )
+    theirs = jnp.concatenate([unpack(got[: half // 2]), got[half // 2 :, :width]], axis=0)
+    rows = jnp.concatenate(
+        [jnp.where(first, mine, theirs), jnp.where(first, theirs, mine)], axis=1
+    )
+    rows_ref[...] = rows
+    quarter = keep_ref.shape[2]
+    for chip in range(2):
+        even, odd = [
+            dot32(rows, weights[0, i * quarter : (i + 1) * quarter, :], NT).astype(BF16)
+            for i in (2 * chip, 2 * chip + 1)
+        ]
+        keep_ref[chip] = jnp.where(low_core, even, odd)
+        send_ref[chip] = jnp.where(low_core, odd, even)
+
+
+def output_grad_kernel(meta, back_ref, rows_ref, keep_ref, send_ref):
+    parts, rows = keep_ref.shape[:2]
+    count = back_ref.shape[0]
+    first = meta[0] == 0
+    mixed = rows_ref[:count]
+    for part in range(parts):
+        cols = slice(part * 2 * rows, (part + 1) * 2 * rows)
+        grad = dot32(back_ref[:, cols], mixed, TN).astype(BF16)
+        keep_ref[part] = jnp.where(first, grad[:rows], grad[rows:])
+        send_ref[part] = jnp.where(first, grad[rows:], grad[:rows])
+
+
+def pack_terms(array):
+    width = array.shape[1] * 2 // 3
+    return jnp.concatenate([array[:, :width], pack(array[:, width:])], axis=0)
+
+
+def unpack_terms(array, rows):
+    return jnp.concatenate([array[:rows], unpack(array[rows:])], axis=1)
+
+
+def terms_kernel(meta, source, mine, across, beside, corner, own, far, away_ref, home_ref, *, shard):
+    first = meta[0] == 0
+    rows = shard // 2
+    grads = jnp.concatenate([own[...], far[...]], axis=0)
+    for step in range(away_ref.shape[0]):
+        start = pl.multiple_of(meta[2 + step] * shard, LANES)
+        piece = meta[2 + step] ^ meta[1]
+        near = source[:, pl.ds(start, shard)]
+        low = jnp.where(piece == 0, mine[...], across[...])
+        high = jnp.where(piece == 2, beside[...], corner[...])
+        frames = jnp.concatenate([near, jnp.where(piece < 2, low, high)], axis=0)
+        chunk = dot32(frames, grads, TN).astype(BF16)
+        away_ref[step] = pack_terms(jnp.where(first, chunk[rows:], chunk[:rows]))
+        home_ref[step] = pack_terms(jnp.where(first, chunk[:rows], chunk[rows:]))
+
+
+def conv_kernel(
+    meta, mine, far, keep, got, up_ref, taps_ref, out_ref, grad_ref, padded, wide, sums
+):
+    count, width = mine.shape
+    step = conv_rows(count)
+    upper = meta[0] == 1
+    for chunk in range(width // LANES):
+        cols = slice(chunk * LANES, (chunk + 1) * LANES)
+        where = pl.ds(pl.multiple_of(meta[1] * width + chunk * LANES, LANES), LANES)
+        edge = jnp.where(upper, far[count - EDGE :, cols], far[:EDGE, cols])
+        frames = jnp.concatenate([mine[:, cols], edge], axis=0)
+        total = frames.astype(F32) + keep[:, cols] + got[:, cols].astype(F32)
+        rows = total.astype(BF16).astype(F32)
+        fill_padded(padded, rows[:count], rows[count:], upper)
+        fill_taps(wide, taps_ref[:, where].astype(F32))
+        sums[...] = jnp.zeros_like(sums)
+
+        def body(tile, carry, cols=cols, where=where):
+            start = pl.multiple_of(tile * step, step)
+            total = padded[pl.ds(start + EDGE, step)]
+            upstream = up_ref[pl.ds(start, step), where].astype(F32)
+            for phase in range(8):
+                loaded = padded[pl.ds(start + phase, step + KW - 8)]
+                for block in range(KW // 8):
+                    offset = phase + 8 * block
+                    shifted = loaded[8 * block : 8 * block + step]
+                    total = tapped(total, wide, offset, shifted)
+                    product = (upstream * shifted).reshape(step // 8, 8, LANES)
+                    sums[offset] = sums[offset] + jnp.sum(product, axis=0)
+            out_ref[pl.ds(start, step), cols] = total.astype(BF16)
+            return carry
+
+        lax.fori_loop(0, count // step, body, 0)
+        grad_ref[:, cols] = jnp.sum(sums[...], axis=1)
+
+
+def final_kernel(meta, home, got, last, out_ref):
+    rows, width = (out_ref.shape[1], out_ref.shape[2] // 2)
+    first = meta[0] == 0
+    mine, theirs = [unpack_terms(x[...], rows) for x in (home, got)]
+    left = jnp.where(first, mine, theirs).astype(F32)
+    right = jnp.where(first, theirs, mine).astype(F32)
+    for i in range(3):
+        cols = slice(i * width, (i + 1) * width)
+        out_ref[i] = jnp.concatenate([left[:, cols], right[:, cols]], axis=1)
+    out_ref[3] = last[...].astype(F32)
+
+
+def place_kernel(meta, mine, across, beside, corner, out_ref):
+    width = mine.shape[1]
+    for i, piece in enumerate((mine, across, beside, corner)):
+        start = pl.multiple_of((meta[1] ^ i) * width, LANES)
+        out_ref[:, pl.ds(start, width)] = piece[...]
+
+
+SIDE = [(0, 1), (1, 0)]
+CORE = [(0, 1), (1, 0), (2, 3), (3, 2)]
+CHIP = [(0, 2), (2, 0), (1, 3), (3, 1)]
+CROSS = [(0, 3), (3, 0), (1, 2), (2, 1)]
+
+
+def columns(array, index, width):
+    return lax.dynamic_slice_in_dim(array, index * width, width, axis=1)
+
+
+def live_bias(pattern, far_pattern, side, local):
+    order = jnp.concatenate(
+        [side * local + jnp.arange(local), (1 - side) * local + jnp.arange(local)]
+    ).astype(jnp.int32)
+    chosen = jnp.concatenate([pattern, far_pattern], axis=0)
+    near = jnp.abs(order[:, None] - order[None, :]) <= 1
+    listed = jnp.any(chosen[None, :, :] == order[:, None, None], axis=-1)
+    bias = jnp.where(near | listed, 0.0, -1e30).astype(jnp.float32)
+    return jnp.repeat(bias, BLK, axis=1)
+
+
+def split_heads(frames, projections, kernel, pattern, cotangent):
+    return split_heads_body(frames[0], projections, kernel, pattern[0], cotangent[0])
+
+
+def split_heads_body(source, projections, kernel, pattern, upstream):
+    count, width = source.shape
+    local = count // BLK
+    ring = lax.axis_size("dp")
+    head_width = projections.shape[2]
+    mine_width = head_width // 2
+    quarter = width // 4
+    shard = width // ring
+    rows = shard // 2
+    side, head, place = (lax.axis_index("tm"), lax.axis_index("head"), lax.axis_index("dp"))
+    first = side == 0
+
+    def chunk_index(step):
+        return (place + (2 * ring - 1 - step)) % ring
+
+    order = [chunk_index(step) for step in range(ring)]
+    meta = jnp.stack([side, head] + order).astype(jnp.int32)
+    later = jnp.stack([side, head] + order[1:]).astype(jnp.int32)
+
+    payload = jnp.concatenate(
+        [
+            jnp.where(first, upstream[count - EDGE :], upstream[:EDGE]),
+            jnp.pad(
+                pattern.astype(BF16),
+                ((0, EDGE - local), (0, LANES - pattern.shape[1])),
+                constant_values=-1,
+            ),
+        ],
+        axis=1,
+    )
+    arrived = lax.ppermute(payload, "tm", SIDE)
+    far_pattern = arrived[:local, width : width + pattern.shape[1]].astype(jnp.int32)
+    frames_mine = columns(source, head, quarter)
+    far_mine = lax.ppermute(frames_mine, "tm", SIDE)
+
+    own, send = project(meta, source, projections)
+    far = lax.ppermute(send, "tm", SIDE)
+    bias = live_bias(pattern, far_pattern, side, local)
+
+    far_across = lax.ppermute(far_mine, "head", CORE)
+    far_beside = lax.ppermute(far_mine, "head", CHIP)
+    far_corner = lax.ppermute(far_beside, "head", CORE)
+    back_grad, grad_own, grad_send = back_conv(meta, upstream, arrived, kernel, projections)
+    grad_far = lax.ppermute(grad_send, "tm", SIDE)
+
+    pairs = (2 * count) ** 2 * (mine_width // HD)
+    mixed_own, mixed_far, mixed_send, logsum = run(
+        forward_kernel,
+        (
+            shape(count, mine_width),
+            shape(count, mine_width),
+            shape(count // 2 + EDGE, head_width),
+            shape(8, 2 * count, dtype=F32),
+        ),
+        4 * pairs * HD,
+        meta,
+        bias,
+        own,
+        far,
+    )
+    mixed_got = lax.ppermute(mixed_send, "tm", SIDE)
+    terms_own, terms_far = run(
+        backward_kernel,
+        (shape(count, 3 * mine_width), shape(count, 3 * mine_width)),
+        10 * pairs * HD,
+        meta,
+        bias,
+        logsum,
+        own,
+        far,
+        grad_own,
+        grad_far,
+        mixed_own,
+        mixed_far,
+    )
+
+    onward = [(i, (i + 1) % ring) for i in range(ring)]
+    packed = rows * 3 // 2
+
+    def ring_terms(numbers, steps):
+        return run(
+            functools.partial(terms_kernel, shard=shard),
+            (shape(steps, packed, shard), shape(steps, packed, shard)),
+            12 * steps * count * shard * mine_width,
+            numbers,
+            source,
+            far_mine,
+            far_across,
+            far_beside,
+            far_corner,
+            terms_own,
+            terms_far,
+        )
+
+    away, home = [x[0] for x in ring_terms(meta, 1)]
+    away_terms, home_terms = ring_terms(later, ring - 1)
+    for step in range(1, ring):
+        away_got = lax.ppermute(away, "dp", onward)
+        home_got = lax.ppermute(home, "dp", onward)
+        away = (away_terms[step - 1].astype(F32) + away_got.astype(F32)).astype(BF16)
+        home_got, _ = lax.optimization_barrier((home_got, away))
+        home = (home_terms[step - 1].astype(F32) + home_got.astype(F32)).astype(BF16)
+    swap_got = lax.ppermute(away, "tm", SIDE)
+
+    whole = pl.BlockSpec(memory_space=pltpu.VMEM)
+    mixed_rows, core_keep, core_send = run(
+        output_kernel,
+        (
+            shape(count + EDGE, head_width),
+            shape(2, count + EDGE, quarter),
+            shape(2, count + EDGE, quarter),
+        ),
+        2 * count * width * head_width,
+        meta,
+        mixed_own,
+        mixed_far,
+        mixed_got,
+        projections,
+        grid=(1,),
+        in_specs=[pl.BlockSpec(memory_space=pltpu.SMEM)]
+        + [whole] * 3
+        + [pl.BlockSpec((1, width, head_width), lambda i: (3, 0, 0))],
+        out_specs=(whole, whole, whole),
+    )
+    core_got = lax.ppermute(core_send, "head", CORE)
+    out_keep, out_send = run(
+        output_grad_kernel,
+        (shape(ring, rows, head_width), shape(ring, rows, head_width)),
+        2 * count * width * head_width,
+        meta,
+        back_grad,
+        mixed_rows,
+    )
+    out_got = lax.ppermute(out_send, "tm", SIDE)
+
+    def out_term(step):
+        kept, came = [
+            lax.dynamic_index_in_dim(x, order[step], 0, keepdims=False).astype(F32)
+            for x in (out_keep, out_got)
+        ]
+        return kept + came
+
+    out_chunk = out_term(0).astype(BF16)
+    for step in range(1, ring):
+        out_arrived = lax.ppermute(out_chunk, "dp", onward)
+        out_chunk = (out_term(step) + out_arrived.astype(F32)).astype(BF16)
+
+    low_chip = head // 2 == 0
+    sums = core_keep.astype(F32) + core_got.astype(F32)
+    chip_keep = jnp.where(low_chip, sums[0], sums[1])
+    chip_send = jnp.where(low_chip, sums[1], sums[0]).astype(BF16)
+    chip_got = lax.ppermute(chip_send, "head", CHIP)
+    encoded, taps_grad = run(
+        conv_kernel,
+        (shape(count, quarter), shape(KW, quarter, dtype=F32)),
+        160 * KW * count * quarter,
+        meta,
+        frames_mine,
+        far_mine,
+        chip_keep,
+        chip_got,
+        upstream,
+        kernel,
+        scratch_shapes=[
+            pltpu.VMEM((count + KW + 8, LANES), F32),
+            pltpu.VMEM((KW, 8, LANES), F32),
+            pltpu.VMEM((KW, 8, LANES), F32),
+        ],
+    )
+
+    tap_rows = KW // (2 * ring)
+    grouped = taps_grad.reshape(ring, 2, tap_rows, quarter)
+    tap_keep = jnp.where(first, grouped[:, 0], grouped[:, 1])
+    tap_send = jnp.where(first, grouped[:, 1], grouped[:, 0])
+    tap_sum = tap_keep + lax.ppermute(tap_send, "tm", SIDE)
+    tap_total = lax.dynamic_index_in_dim(tap_sum, place, 0, keepdims=False)
+    for hop in range(1, ring):
+        leaving = lax.dynamic_index_in_dim(tap_sum, (place + hop) % ring, 0, keepdims=False)
+        tap_total = tap_total + lax.ppermute(
+            leaving, "dp", [(i, (i + hop) % ring) for i in range(ring)]
+        )
+    pieces = [tap_total]
+    for group in (CORE, CHIP, CROSS):
+        pieces.append(lax.ppermute(tap_total, "head", group))
+    kernel_result = jnp.concatenate(
+        [lax.select_n((head ^ i).astype(jnp.int32), *pieces) for i in range(4)], axis=1
+    )
+    beside = lax.ppermute(encoded, "head", CHIP)
+    across = lax.ppermute(encoded, "head", CORE)
+    corner = lax.ppermute(beside, "head", CORE)
+    encoded_all = run(place_kernel, shape(count, width), 0, meta, encoded, across, beside, corner)
+    proj_result = run(
+        final_kernel, shape(4, rows, head_width, dtype=F32), 0, meta, home, swap_got, out_chunk
+    )
+    return (encoded_all[None], proj_result, kernel_result)
+
+
 def solution(mesh):
     placed = (
         P("dp", "tm", None),
@@ -224,10 +786,22 @@
         P("dp", "tm", None),
         P("dp", "tm", None),
     )
-    return jax.shard_map(
-        shards,
-        mesh=mesh,
-        in_specs=placed,
-        out_specs=(P("dp", "tm", None), P(None, ("dp", "tm"), "head"), P(("dp", "tm"), None)),
-        check_vma=False,
-    )
+    sizes = dict(mesh.shape)
+    small = sizes["tm"] == 2 and sizes["head"] == 4 and sizes["dp"] == 4
+
+    def chosen(frames, projections, kernel, pattern, cotangent):
+        fits = (
+            small
+            and frames.shape[1] <= 768
+            and projections.shape[2] // 4 == 4 * HD
+            and frames.shape[2] % (4 * LANES) == 0
+        )
+        return jax.shard_map(
+            split_heads if fits else shards,
+            mesh=mesh,
+            in_specs=placed,
+            out_specs=(P("dp", "tm", None), P(None, ("dp", "tm"), "head"), P(("dp", "tm"), None)),
+            check_vma=False,
+        )(frames, projections, kernel, pattern, cotangent)
+
+    return chosen

time: 492 us -> 137 us (0.28)
  waiting for transfers between devices: 190 us -> 38.9 us
  local copies, waits for them, and re-layouts: 128 us -> 19.8 us
  matrix products: 63.8 us -> 0 us
  other arithmetic: 63.5 us -> 8.11 us
  Pallas kernels: 0 us -> 38.6 us
  starting transfers between devices: 4.96 us -> 30 us
  blocking collectives: 19.9 us -> 0 us
  between operations: 17.2 us -> 1.13 us
    unnamed x4 -> x0, waiting for transfers between devices: 149 us -> none
    dot_general x17 -> x0, matrix products: 63.8 us -> none  [the longest x1 8.5 us: attend_back(): jnp.einsum('qhtk,qthd->qkhd', weights, grad_tiles, preferred_element_type...]
    pallas_call x0 -> x11, Pallas kernels: none -> 38.6 us  [run(): pl.pallas_call(body, out_shape=outs, compiler_params=pltpu.CompilerParams...]
    reshape x12 -> x2, local copies, waits for them, and re-layouts: 38.1 us -> 0.1 us  [the longest x1 0.08 us: live_bias(): return jnp.repeat(bias, BLK, axis=1)]
    psum x1 -> x0, waiting for transfers between devices: 36.6 us -> none  [shards(): lax.psum(output_part.astype(jnp.bfloat16), 'head').astype(jnp.float32)]
    ppermute x2 -> x31, waiting for transfers between devices: 4.85 us -> 38.9 us  [the longest x1 10 us: split_heads_body(): arrived = lax.ppermute(payload, 'tm', SIDE)]
    another operation x34 -> x2, local copies, waits for them, and re-layouts: 33.5 us -> 0.17 us  [the longest x1 0.09 us: split_heads_body(): meta = jnp.stack([side, head] + order).astype(jnp.int32)]
    transpose x2 -> x0, local copies, waits for them, and re-layouts: 26.5 us -> none  [the longest x1 13.3 us: attend_back(): jnp.einsum('qhtk,qthd->qkhd', weights, grad_tiles, preferred_element_type...]
  transfers between devices with their start and end apart: 5 -> 31, of which waited for: 4 -> 13; matrix products, arithmetic and copies ran while one was open for 13% -> 6% of each run, Pallas kernels for 0% -> 24%
where the time goes in v1:
time: 137 us
  waiting for transfers between devices  38.9 us (28%)
  Pallas kernels  38.6 us (28%)
  starting transfers between devices  30 us (22%)
  local copies, waits for them, and re-layouts  19.8 us (14%)
  other arithmetic  8.11 us (6%)
    pallas_call x11, Pallas kernels, run(): pl.pallas_call(body, out_shape=outs, compiler_params=pltpu.CompilerParams...  38.6 us
    unnamed x74, local copies, waits for them, and re-layouts  19.4 us
    ppermute x1, waiting for transfers between devices, split_heads_body(): arrived = lax.ppermute(payload, 'tm', SIDE)  10 us
    ppermute x3, waiting for transfers between devices, split_heads_body(): out_arrived = lax.ppermute(out_chunk, 'dp', onward)  9.29 us
    ppermute x1, waiting for transfers between devices, split_heads_body(): far_beside = lax.ppermute(far_mine, 'head', CHIP)  4.75 us
    ppermute x3, starting transfers between devices, split_heads_body(): away_got = lax.ppermute(away, 'dp', onward)  4.42 us
    ppermute x3, starting transfers between devices, split_heads_body(): lax.ppermute(leaving, 'dp', [(i, (i + hop) % ring) for i in range(ring)])  4.42 us
    ppermute x1, waiting for transfers between devices, split_heads_body(): swap_got = lax.ppermute(away, 'tm', SIDE)  4.2 us
  transfers between devices with their start and end apart: 31, of which 13 were waited for; matrix products, arithmetic and copies ran while one was open for 6% of the time, Pallas kernels for 24%

profile of v1, /device:TPU:0, one launch (start us, length us, event | category | flops | bytes accessed | tf_op | source)
XLA Modules:
  0.0 136.6 jit_solution(10744961505708151642)
XLA Ops:
  0.8 2.3 %copy-done = bf16[4,1536,384]{2,1,0:T(8,128)(2,1)S(1)} copy-done((bf16[4,1536,384]{2,1,0:T(8,128)(2,1)S(1)}, bf16[4,1536,384]{2,1,0:T(8,128)(2,1)}, u32[]{:S(2)}) %copy-start) | copy-done | bytes 4718616
  4.4 3.9 %shard_map.76 = (bf16[3,384,192]{2,1,0:T(8,128)(2,1)S(1)}, bf16[3,192,384]{2,1,0:T(8,128)(2,1)}) custom-call(s32[6]{0:T(128)S(1)} %stack.35.meta, bf16[384,1536]{1,0:T(8,128)(2,1)S(1)} %bitcast.87, bf16[4,1536,384]{2,1,0:T(8,128)(2,1)S(1)} %copy-done), custom_call_target="tpu_custom_call" | custom-call | flops 1358954496 | bytes 5898264 | tf_op jit(solution)/shard_map/pallas_call | solution.py:246
  9.1 3.0 %collective-permute-start.2 = (bf16[3,192,384]{2,1,0:T(8,128)(2,1)}, bf16[3,192,384]{2,1,0:T(8,128)(2,1)}, u32[]{:S(2)}, u32[]{:S(2)}) collective-permute-start(bf16[3,192,384]{2,1,0:T(8,128)(2,1)} %get-tuple-element.29), channel_id=1, source_target_pairs={{0,4},{4,0},{1,5},{5,1},{2,6},{6,2},{3,7},{7,3},{8,12},{12,8},{9,1... | collective-permute-start | bytes 1327112 | tf_op jit(solution)/shard_map/ppermute | solution.py:620
  12.2 2.1 %collective-permute-start = (bf16[384,384]{1,0:T(8,128)(2,1)S(1)}, bf16[384,384]{1,0:T(8,128)(2,1)S(1)}, u32[]{:S(2)}, u32[]{:S(2)}) collective-permute-start(bf16[384,384]{1,0:T(8,128)(2,1)S(1)} %dynamic-slice_bitcast_fusion.mine), channel_id=1, source_target_pairs={{0,4},{4,0},{1,5},{5,1},{2,6},{6,2},{3,7},{7,3},{8,12},{12,8},{9,1... | collective-permute-start | bytes 884744 | tf_op jit(solution)/shard_map/ppermute | solution.py:617
  14.4 10.0 %collective-permute-done.1.arrived = bf16[16,1664]{1,0:T(8,128)(2,1)S(1)} collective-permute-done((bf16[16,1664]{1,0:T(8,128)(2,1)S(1)}, bf16[16,1664]{1,0:T(8,128)(2,1)S(1)}, u32[]{:S(2)}, u32[]{:S(2)}) %collective-permute-start.1) | collective-permute-done | bytes 53280 | tf_op jit(solution)/shard_map/ppermute | solution.py:614
  25.0 2.3 %copy-done.1 = bf16[4,1536,384]{2,1,0:T(8,128)(2,1)S(1)} copy-done((bf16[4,1536,384]{2,1,0:T(8,128)(2,1)S(1)}, bf16[4,1536,384]{2,1,0:T(8,128)(2,1)}, u32[]{:S(2)}) %copy-start.1) | copy-done | bytes 4718616
  29.1 9.7 %shard_map.81 = (bf16[384,1536]{1,0:T(8,128)(2,1)S(1)}, bf16[384,192]{1,0:T(8,128)(2,1)S(1)}, bf16[192,384]{1,0:T(8,128)(2,1)}) custom-call(s32[6]{0:T(128)S(1)} %stack.35.meta, bf16[384,1536]{1,0:T(8,128)(2,1)S(1)} %bitcast.90, bf16[16,1664]{1,0:T(8,128)(2,1)S(1)} %copy-done.24, bf16[32,1536]{1,0:T(8,128)(2,1)S(1)} %copy-done.28, ...), custom_call_target="tpu_custom_call" | custom-call | flops 1962934272 | bytes 6049816 | tf_op jit(solution)/shard_map/pallas_call | solution.py:246
  40.5 2.0 %collective-permute-start.12 = (bf16[192,384]{1,0:T(8,128)(2,1)}, bf16[192,384]{1,0:T(8,128)(2,1)}, u32[]{:S(2)}, u32[]{:S(2)}) collective-permute-start(bf16[192,384]{1,0:T(8,128)(2,1)} %get-tuple-element.38), channel_id=1, source_target_pairs={{0,4},{4,0},{1,5},{5,1},{2,6},{6,2},{3,7},{7,3},{8,12},{12,8},{9,1... | collective-permute-start | bytes 442376 | tf_op jit(solution)/shard_map/ppermute | solution.py:627
  44.5 4.8 %collective-permute-done.10.beside = bf16[384,384]{1,0:T(8,128)(2,1)S(1)} collective-permute-done((bf16[384,384]{1,0:T(8,128)(2,1)S(1)}, bf16[384,384]{1,0:T(8,128)(2,1)S(1)}, u32[]{:S(2)}, u32[]{:S(2)}) %collective-permute-start.10) | collective-permute-done | bytes 294944 | tf_op jit(solution)/shard_map/ppermute | solution.py:624
  50.6 4.2 %shard_map.77 = (bf16[384,192]{1,0:T(8,128)(2,1)S(1)}, bf16[384,192]{1,0:T(8,128)(2,1)S(1)}, bf16[208,384]{1,0:T(8,128)(2,1)S(1)}, f32[8,768]{1,0:T(8,128)S(1)}) custom-call(s32[6]{0:T(128)S(1)} %stack.35.meta, f32[12,768]{1,0:T(8,128)S(1)} %reshape.55.bias_ref, bf16[3,384,192]{2,1,0:T(8,128)(2,1)S(1)} %copy-done.26, ...), custom_call_target="tpu_custom_call" | custom-call | flops 452984832 | bytes 921624 | tf_op jit(solution)/shard_map/pallas_call | solution.py:246
  57.2 4.9 %shard_map.82 = (bf16[384,576]{1,0:T(8,128)(2,1)S(1)}, bf16[384,576]{1,0:T(8,128)(2,1)S(1)}) custom-call(s32[6]{0:T(128)S(1)} %stack.35.meta, f32[12,768]{1,0:T(8,128)S(1)} %reshape.55.bias_ref, f32[8,768]{1,0:T(8,128)S(1)} %get-tuple-element.36.logsum_ref, bf16[3,384,192]{2,1,0:T(8,128)(2,1)S(1)} %copy-done.27, ...), custom_call_target="tpu_custom_call" | custom-call | flops 1132462080 | bytes 1536024 | tf_op jit(solution)/shard_map/pallas_call | solution.py:246
  62.2 2.1 %shard_map.84 = (bf16[1,288,384]{2,1,0:T(8,128)(2,1)}, bf16[1,288,384]{2,1,0:T(8,128)(2,1)}) custom-call(s32[6]{0:T(128)S(1)} %stack.35.meta, bf16[384,1536]{1,0:T(8,128)(2,1)S(1)} %bitcast.88, bf16[384,384]{1,0:T(8,128)(2,1)S(1)} %collective-permute-done.far.mine, bf16[384,384]{1,0:T(8,128)(2,1)S(1)} %collective-permute-done.9.across, ...), custom_call_target="tpu_custom_call" | custom-call | flops 339738624 | bytes 3244056 | tf_op jit(solution)/shard_map/pallas_call | solution.py:246
  64.3 1.9 %collective-permute-start.14 = (bf16[288,384]{1,0:T(8,128)(2,1)}, bf16[288,384]{1,0:T(8,128)(2,1)}, u32[]{:S(2)}, u32[]{:S(2)}) collective-permute-start(bf16[288,384]{1,0:T(8,128)(2,1)} %bitcast.18), channel_id=1, source_target_pairs={{0,8},{8,16},{16,24},{24,0},{1,9},{9,17},{17,25},{25,1},{2,10},{10... | collective-permute-start | bytes 663560 | tf_op jit(solution)/shard_map/ppermute | solution.py:681
  66.3 2.5 %shard_map.78 = (bf16[400,384]{1,0:T(8,128)(2,1)S(1)}, bf16[2,400,384]{2,1,0:T(8,128)(2,1)S(1)}, bf16[2,400,384]{2,1,0:T(8,128)(2,1)}) custom-call(s32[6]{0:T(128)S(1)} %stack.35.meta, bf16[384,192]{1,0:T(8,128)(2,1)S(1)} %get-tuple-element.30.mixed_own, bf16[384,192]{1,0:T(8,128)(2,1)S(1)} %get-tuple-element.31.mixed_far, ...), custom_call_target="tpu_custom_call" | custom-call | flops 452984832 | bytes 5173272 | tf_op jit(solution)/shard_map/pallas_call | solution.py:246
  69.6 2.3 %shard_map.85 = (bf16[4,192,384]{2,1,0:T(8,128)(2,1)S(1)}, bf16[4,192,384]{2,1,0:T(8,128)(2,1)}) custom-call(s32[6]{0:T(128)S(1)} %stack.35.meta, bf16[384,1536]{1,0:T(8,128)(2,1)S(1)} %copy-done.31, bf16[400,384]{1,0:T(8,128)(2,1)S(1)} %get-tuple-element.49.rows_ref), custom_call_target="tpu_custom_call" | custom-call | flops 452984832 | bytes 1486872 | tf_op jit(solution)/shard_map/pallas_call | solution.py:246
  79.9 2.3 %shard_map.83 = (bf16[3,288,384]{2,1,0:T(8,128)(2,1)S(1)}, bf16[3,288,384]{2,1,0:T(8,128)(2,1)S(1)}) custom-call(s32[5]{0:T(128)S(1)} %stack.36.meta, bf16[384,1536]{1,0:T(8,128)(2,1)S(1)} %bitcast.89, bf16[384,384]{1,0:T(8,128)(2,1)S(1)} %copy-done.13, bf16[384,384]{1,0:T(8,128)(2,1)S(1)} %copy-done.18, bf16[384,384]{1,0:T(8,128)(2,1)S(1)} %copy-done.16, ...), custom_call_target="tpu_custom_call" | custom-call | flops 1019215872 | bytes 3244052 | tf_op jit(solution)/shard_map/pallas_call | solution.py:246
  85.2 3.0 %collective-permute-done.20 = bf16[4,192,384]{2,1,0:T(8,128)(2,1)} collective-permute-done((bf16[4,192,384]{2,1,0:T(8,128)(2,1)}, bf16[4,192,384]{2,1,0:T(8,128)(2,1)}, u32[]{:S(2)}, u32[]{:S(2)}) %collective-permute-start.20) | collective-permute-done | bytes 589856 | tf_op jit(solution)/shard_map/ppermute | solution.py:717
  95.1 3.1 %collective-permute-done.15 = bf16[288,384]{1,0:T(8,128)(2,1)S(1)} collective-permute-done((bf16[288,384]{1,0:T(8,128)(2,1)S(1)}, bf16[288,384]{1,0:T(8,128)(2,1)S(1)}, u32[]{:S(2)}, u32[]{:S(2)}) %collective-permute-start.15) | collective-permute-done | bytes 221216 | tf_op jit(solution)/shard_map/ppermute | solution.py:682
  98.3 3.0 %collective-permute-done.21 = bf16[192,384]{1,0:T(8,128)(2,1)S(1)} collective-permute-done((bf16[192,384]{1,0:T(8,128)(2,1)S(1)}, bf16[192,384]{1,0:T(8,128)(2,1)S(1)}, u32[]{:S(2)}, u32[]{:S(2)}) %collective-permute-start.21) | collective-permute-done | bytes 147488 | tf_op jit(solution)/shard_map/ppermute | solution.py:728
  103.0 3.4 %shard_map.79 = (bf16[384,384]{1,0:T(8,128)(2,1)S(1)}, f32[32,384]{1,0:T(8,128)S(1)}) custom-call(s32[6]{0:T(128)S(1)} %stack.35.meta, bf16[384,384]{1,0:T(8,128)(2,1)S(1)} %copy-done.11, bf16[384,384]{1,0:T(8,128)(2,1)S(1)} %copy-done.14, f32[400,384]{1,0:T(8,128)S(1)} %select_bitcast_fusion.keep, bf16[400,384]{1,0:T(8,128)(2,1)S(1)} %collective-permute-done.5.got, ...), custom_call_target="tpu_custom_call" | custom-call | flops 754974720 | bytes 2789400 | tf_op jit(solution)/shard_map/pallas_call | solution.py:246
  107.0 6.3 %collective-permute-done.22 = bf16[192,384]{1,0:T(8,128)(2,1)} collective-permute-done((bf16[192,384]{1,0:T(8,128)(2,1)}, bf16[192,384]{1,0:T(8,128)(2,1)}, u32[]{:S(2)}, u32[]{:S(2)}) %collective-permute-start.22) | collective-permute-done | bytes 147488 | tf_op jit(solution)/shard_map/ppermute | solution.py:728
  114.5 4.3 %collective-permute-start.26 = (f32[4,384]{1,0:T(4,128)S(1)}, f32[4,384]{1,0:T(4,128)S(1)}, u32[]{:S(2)}, u32[]{:S(2)}) collective-permute-start(f32[4,384]{1,0:T(4,128)S(1)} %get-tuple-element.59), channel_id=1, source_target_pairs={{0,16},{8,24},{16,0},{24,8},{1,17},{9,25},{17,1},{25,9},{2,18},{10... | collective-permute-start | bytes 18440 | tf_op jit(solution)/shard_map/ppermute | solution.py:762
  129.0 4.2 %collective-permute-done.19.got = bf16[288,384]{1,0:T(8,128)(2,1)S(1)} collective-permute-done((bf16[288,384]{1,0:T(8,128)(2,1)S(1)}, bf16[288,384]{1,0:T(8,128)(2,1)S(1)}, u32[]{:S(2)}, u32[]{:S(2)}) %collective-permute-start.19) | collective-permute-done | bytes 221216 | tf_op jit(solution)/shard_map/ppermute | solution.py:686
  133.2 1.7 %shard_map.86 = f32[4,192,384]{2,1,0:T(8,128)} custom-call(s32[6]{0:T(128)S(1)} %stack.35.meta, bf16[288,384]{1,0:T(8,128)(2,1)S(1)} %fusion.5.home, bf16[288,384]{1,0:T(8,128)(2,1)S(1)} %collective-permute-done.19.got, bf16[192,384]{1,0:T(8,128)(2,1)S(1)} %fusion.9.last), custom_call_target="tpu_custom_call" | custom-call | bytes 589848 | tf_op jit(solution)/shard_map/pallas_call | solution.py:246
  (158 shorter events, 46.2 us)
Async XLA Ops:
  9.1 40.4 %collective-permute-start.2 = (bf16[3,192,384]{2,1,0:T(8,128)(2,1)}, bf16[3,192,384]{2,1,0:T(8,128)(2,1)}, u32[]{:S(2)}, u32[]{:S(2)}) collective-permute-start(bf16[3,192,384]{2,1,0:T(8,128)(2,1)} %get-tuple-element.29), channel_id=1, source_target_pairs={{0,4},{4,0},{1,5},{5,1},{2,6},{6,2},{3,7},{7,3},{8,12},{12,8},{9,1... | collective-permute-start | bytes 1327112 | tf_op jit(solution)/shard_map/ppermute | solution.py:620
  12.1 12.3 %collective-permute-start.1 = (bf16[16,1664]{1,0:T(8,128)(2,1)S(1)}, bf16[16,1664]{1,0:T(8,128)(2,1)S(1)}, u32[]{:S(2)}, u32[]{:S(2)}) collective-permute-start(bf16[16,1664]{1,0:T(8,128)(2,1)S(1)} %fusion.12), channel_id=1, source_target_pairs={{0,4},{4,0},{1,5},{5,1},{2,6},{6,2},{3,7},{7,3},{8,12},{12,8},{9,1... | collective-permute-start | bytes 159752 | tf_op jit(solution)/shard_map/ppermute | solution.py:614
  12.2 30.3 %collective-permute-start = (bf16[384,384]{1,0:T(8,128)(2,1)S(1)}, bf16[384,384]{1,0:T(8,128)(2,1)S(1)}, u32[]{:S(2)}, u32[]{:S(2)}) collective-permute-start(bf16[384,384]{1,0:T(8,128)(2,1)S(1)} %dynamic-slice_bitcast_fusion.mine), channel_id=1, source_target_pairs={{0,4},{4,0},{1,5},{5,1},{2,6},{6,2},{3,7},{7,3},{8,12},{12,8},{9,1... | collective-permute-start | bytes 884744 | tf_op jit(solution)/shard_map/ppermute | solution.py:617
  40.5 14.8 %collective-permute-start.12 = (bf16[192,384]{1,0:T(8,128)(2,1)}, bf16[192,384]{1,0:T(8,128)(2,1)}, u32[]{:S(2)}, u32[]{:S(2)}) collective-permute-start(bf16[192,384]{1,0:T(8,128)(2,1)} %get-tuple-element.38), channel_id=1, source_target_pairs={{0,4},{4,0},{1,5},{5,1},{2,6},{6,2},{3,7},{7,3},{8,12},{12,8},{9,1... | collective-permute-start | bytes 442376 | tf_op jit(solution)/shard_map/ppermute | solution.py:627
  44.4 17.7 %collective-permute-start.9 = (bf16[384,384]{1,0:T(8,128)(2,1)S(1)}, bf16[384,384]{1,0:T(8,128)(2,1)S(1)}, u32[]{:S(2)}, u32[]{:S(2)}) collective-permute-start(bf16[384,384]{1,0:T(8,128)(2,1)S(1)} %collective-permute-done.far.mine), channel_id=1, source_target_pairs={{0,1},{1,0},{2,3},{3,2},{4,5},{5,4},{6,7},{7,6},{8,9},{9,8},{10,11... | collective-permute-start | bytes 884744 | tf_op jit(solution)/shard_map/ppermute | solution.py:623
  49.2 12.9 %collective-permute-start.11 = (bf16[384,384]{1,0:T(8,128)(2,1)S(1)}, bf16[384,384]{1,0:T(8,128)(2,1)S(1)}, u32[]{:S(2)}, u32[]{:S(2)}) collective-permute-start(bf16[384,384]{1,0:T(8,128)(2,1)S(1)} %collective-permute-done.10.beside), channel_id=1, source_target_pairs={{0,1},{1,0},{2,3},{3,2},{4,5},{5,4},{6,7},{7,6},{8,9},{9,8},{10,11... | collective-permute-start | bytes 884744 | tf_op jit(solution)/shard_map/ppermute | solution.py:625
  54.7 11.5 %collective-permute-start.3 = (bf16[208,384]{1,0:T(8,128)(2,1)S(1)}, bf16[208,384]{1,0:T(8,128)(2,1)S(1)}, u32[]{:S(2)}, u32[]{:S(2)}) collective-permute-start(bf16[208,384]{1,0:T(8,128)(2,1)S(1)} %get-tuple-element.32), channel_id=1, source_target_pairs={{0,4},{4,0},{1,5},{5,1},{2,6},{6,2},{3,7},{7,3},{8,12},{12,8},{9,1... | collective-permute-start | bytes 479240 | tf_op jit(solution)/shard_map/ppermute | solution.py:644
  64.3 17.8 %collective-permute-start.14 = (bf16[288,384]{1,0:T(8,128)(2,1)}, bf16[288,384]{1,0:T(8,128)(2,1)}, u32[]{:S(2)}, u32[]{:S(2)}) collective-permute-start(bf16[288,384]{1,0:T(8,128)(2,1)} %bitcast.18), channel_id=1, source_target_pairs={{0,8},{8,16},{16,24},{24,0},{1,9},{9,17},{17,25},{25,1},{2,10},{10... | collective-permute-start | bytes 663560 | tf_op jit(solution)/shard_map/ppermute | solution.py:681
  72.7 15.5 %collective-permute-start.20 = (bf16[4,192,384]{2,1,0:T(8,128)(2,1)}, bf16[4,192,384]{2,1,0:T(8,128)(2,1)}, u32[]{:S(2)}, u32[]{:S(2)}) collective-permute-start(bf16[4,192,384]{2,1,0:T(8,128)(2,1)} %get-tuple-element.51), channel_id=1, source_target_pairs={{0,4},{4,0},{1,5},{5,1},{2,6},{6,2},{3,7},{7,3},{8,12},{12,8},{9,1... | collective-permute-start | bytes 1769480 | tf_op jit(solution)/shard_map/ppermute | solution.py:717
  74.3 16.5 %collective-permute-start.4 = (bf16[2,400,384]{2,1,0:T(8,128)(2,1)}, bf16[2,400,384]{2,1,0:T(8,128)(2,1)S(1)}, u32[]{:S(2)}, u32[]{:S(2)}) collective-permute-start(bf16[2,400,384]{2,1,0:T(8,128)(2,1)} %get-tuple-element.34), channel_id=1, source_target_pairs={{0,1},{1,0},{2,3},{3,2},{4,5},{5,4},{6,7},{7,6},{8,9},{9,8},{10,11... | collective-permute-start | bytes 1843208 | tf_op jit(solution)/shard_map/ppermute | solution.py:708
  74.4 10.5 %collective-permute-start.13 = (bf16[288,384]{1,0:T(8,128)(2,1)}, bf16[288,384]{1,0:T(8,128)(2,1)S(1)}, u32[]{:S(2)}, u32[]{:S(2)}) collective-permute-start(bf16[288,384]{1,0:T(8,128)(2,1)} %bitcast.16), channel_id=1, source_target_pairs={{0,8},{8,16},{16,24},{24,0},{1,9},{9,17},{17,25},{25,1},{2,10},{10... | collective-permute-start | bytes 663560 | tf_op jit(solution)/shard_map/ppermute | solution.py:682
  83.3 10.1 %collective-permute-start.16 = (bf16[288,384]{1,0:T(8,128)(2,1)S(1)}, bf16[288,384]{1,0:T(8,128)(2,1)S(1)}, u32[]{:S(2)}, u32[]{:S(2)}) collective-permute-start(bf16[288,384]{1,0:T(8,128)(2,1)S(1)} %fusion.2), channel_id=1, source_target_pairs={{0,8},{8,16},{16,24},{24,0},{1,9},{9,17},{17,25},{25,1},{2,10},{10... | collective-permute-start | bytes 663560 | tf_op jit(solution)/shard_map/ppermute | solution.py:681
  85.0 13.2 %collective-permute-start.15 = (bf16[288,384]{1,0:T(8,128)(2,1)S(1)}, bf16[288,384]{1,0:T(8,128)(2,1)S(1)}, u32[]{:S(2)}, u32[]{:S(2)}) collective-permute-start(bf16[288,384]{1,0:T(8,128)(2,1)S(1)} %fusion.3), channel_id=1, source_target_pairs={{0,8},{8,16},{16,24},{24,0},{1,9},{9,17},{17,25},{25,1},{2,10},{10... | collective-permute-start | bytes 663560 | tf_op jit(solution)/shard_map/ppermute | solution.py:682
  89.2 12.1 %collective-permute-start.21 = (bf16[192,384]{1,0:T(8,128)(2,1)S(1)}, bf16[192,384]{1,0:T(8,128)(2,1)S(1)}, u32[]{:S(2)}, u32[]{:S(2)}) collective-permute-start(bf16[192,384]{1,0:T(8,128)(2,1)S(1)} %fusion.10), channel_id=1, source_target_pairs={{0,8},{8,16},{16,24},{24,0},{1,9},{9,17},{17,25},{25,1},{2,10},{10... | collective-permute-start | bytes 442376 | tf_op jit(solution)/shard_map/ppermute | solution.py:728
  91.0 11.9 %collective-permute-start.5 = (bf16[400,384]{1,0:T(8,128)(2,1)S(1)}, bf16[400,384]{1,0:T(8,128)(2,1)S(1)}, u32[]{:S(2)}, u32[]{:S(2)}) collective-permute-start(bf16[400,384]{1,0:T(8,128)(2,1)S(1)} %fusion.6), channel_id=1, source_target_pairs={{0,2},{2,0},{1,3},{3,1},{4,6},{6,4},{5,7},{7,5},{8,10},{10,8},{9,1... | collective-permute-start | bytes 921608 | tf_op jit(solution)/shard_map/ppermute | solution.py:735
  94.2 24.7 %collective-permute-start.18 = (bf16[288,384]{1,0:T(8,128)(2,1)}, bf16[288,384]{1,0:T(8,128)(2,1)S(1)}, u32[]{:S(2)}, u32[]{:S(2)}) collective-permute-start(bf16[288,384]{1,0:T(8,128)(2,1)} %fusion.1), channel_id=1, source_target_pairs={{0,8},{8,16},{16,24},{24,0},{1,9},{9,17},{17,25},{25,1},{2,10},{10... | collective-permute-start | bytes 663560 | tf_op jit(solution)/shard_map/ppermute | solution.py:681
  98.2 20.7 %collective-permute-start.17 = (bf16[288,384]{1,0:T(8,128)(2,1)S(1)}, bf16[288,384]{1,0:T(8,128)(2,1)S(1)}, u32[]{:S(2)}, u32[]{:S(2)}) collective-permute-start(bf16[288,384]{1,0:T(8,128)(2,1)S(1)} %fusion.4), channel_id=1, source_target_pairs={{0,8},{8,16},{16,24},{24,0},{1,9},{9,17},{17,25},{25,1},{2,10},{10... | collective-permute-start | bytes 663560 | tf_op jit(solution)/shard_map/ppermute | solution.py:682
  102.9 10.3 %collective-permute-start.22 = (bf16[192,384]{1,0:T(8,128)(2,1)}, bf16[192,384]{1,0:T(8,128)(2,1)}, u32[]{:S(2)}, u32[]{:S(2)}) collective-permute-start(bf16[192,384]{1,0:T(8,128)(2,1)} %fusion.7), channel_id=1, source_target_pairs={{0,8},{8,16},{16,24},{24,0},{1,9},{9,17},{17,25},{25,1},{2,10},{10... | collective-permute-start | bytes 442376 | tf_op jit(solution)/shard_map/ppermute | solution.py:728
  106.4 8.0 %collective-permute-start.24 = (f32[4,4,384]{2,1,0:T(4,128)S(1)}, f32[4,4,384]{2,1,0:T(4,128)S(1)}, u32[]{:S(2)}, u32[]{:S(2)}) collective-permute-start(f32[4,4,384]{2,1,0:T(4,128)S(1)} %select_bitcast_fusion.2), channel_id=1, source_target_pairs={{0,4},{4,0},{1,5},{5,1},{2,6},{6,2},{3,7},{7,3},{8,12},{12,8},{9,1... | collective-permute-start | bytes 73736 | tf_op jit(solution)/shard_map/ppermute | solution.py:758
  114.3 13.7 %collective-permute-start.23 = (bf16[192,384]{1,0:T(8,128)(2,1)S(1)}, bf16[192,384]{1,0:T(8,128)(2,1)S(1)}, u32[]{:S(2)}, u32[]{:S(2)}) collective-permute-start(bf16[192,384]{1,0:T(8,128)(2,1)S(1)} %fusion.8), channel_id=1, source_target_pairs={{0,8},{8,16},{16,24},{24,0},{1,9},{9,17},{17,25},{25,1},{2,10},{10... | collective-permute-start | bytes 442376 | tf_op jit(solution)/shard_map/ppermute | solution.py:728
  114.5 7.2 %collective-permute-start.26 = (f32[4,384]{1,0:T(4,128)S(1)}, f32[4,384]{1,0:T(4,128)S(1)}, u32[]{:S(2)}, u32[]{:S(2)}) collective-permute-start(f32[4,384]{1,0:T(4,128)S(1)} %get-tuple-element.59), channel_id=1, source_target_pairs={{0,16},{8,24},{16,0},{24,8},{1,17},{9,25},{17,1},{25,9},{2,18},{10... | collective-permute-start | bytes 18440 | tf_op jit(solution)/shard_map/ppermute | solution.py:762
  118.9 8.2 %collective-permute-start.7 = (bf16[384,384]{1,0:T(8,128)(2,1)S(1)}, bf16[384,384]{1,0:T(8,128)(2,1)S(1)}, u32[]{:S(2)}, u32[]{:S(2)}) collective-permute-start(bf16[384,384]{1,0:T(8,128)(2,1)S(1)} %get-tuple-element.35.mine), channel_id=1, source_target_pairs={{0,2},{2,0},{1,3},{3,1},{4,6},{6,4},{5,7},{7,5},{8,10},{10,8},{9,1... | collective-permute-start | bytes 884744 | tf_op jit(solution)/shard_map/ppermute | solution.py:771
  124.4 10.5 %collective-permute-start.6 = (bf16[384,384]{1,0:T(8,128)(2,1)S(1)}, bf16[384,384]{1,0:T(8,128)(2,1)S(1)}, u32[]{:S(2)}, u32[]{:S(2)}) collective-permute-start(bf16[384,384]{1,0:T(8,128)(2,1)S(1)} %get-tuple-element.35.mine), channel_id=1, source_target_pairs={{0,1},{1,0},{2,3},{3,2},{4,5},{5,4},{6,7},{7,6},{8,9},{9,8},{10,11... | collective-permute-start | bytes 884744 | tf_op jit(solution)/shard_map/ppermute | solution.py:772
  127.1 7.7 %collective-permute-start.8 = (bf16[384,384]{1,0:T(8,128)(2,1)S(1)}, bf16[384,384]{1,0:T(8,128)(2,1)S(1)}, u32[]{:S(2)}, u32[]{:S(2)}) collective-permute-start(bf16[384,384]{1,0:T(8,128)(2,1)S(1)} %collective-permute-done.7.beside), channel_id=1, source_target_pairs={{0,1},{1,0},{2,3},{3,2},{4,5},{5,4},{6,7},{7,6},{8,9},{9,8},{10,11... | collective-permute-start | bytes 884744 | tf_op jit(solution)/shard_map/ppermute | solution.py:773
  (44 other events, 261.9 us)
